TPU v7x, 256 devices: a whole 4x4x8 slice. The times are simulated.
256 devices in a mesh: head: 8 (over z), seq: 32 (over y, x, core).
Axes of the slice: x: 4, y: 4, z: 8, core: 2. Of those that a mesh axis runs over, the one named last changes fastest.
Arguments:
- tokens: bfloat16 [32768, 4096], P('seq')
- qkv_weight: bfloat16 [4096, 6144], P('seq', 'head'), may hold values from -0.09375 to 0.09375
- out_weight: bfloat16 [2048, 4096], P('head', 'seq'), may hold values from -0.125 to 0.125
- centroids: float32 [16, 256, 128], P('head', 'seq'), may hold values from -6 to 6
- clusters: int32 [16, 256], P('head', 'seq'), may hold values from 0 to 255, as said below
- slots: int32 [16, 256], P('head', 'seq'), may hold values from 0 to 1, as said below
Outputs:
- output: bfloat16 [4096, 32768], P('head', 'seq')
- new_centroids: float32 [16, 256, 128], P('head', 'seq')
Inputs may be any that keep to these rules, and one draw needn't show every extreme that they name: `clusters`: for each head at most 2 tiles name one cluster, and in each head every cluster of some owner holds 2 tiles; the owner of cluster c is the index c // 8 of seq. A tile of head h from the index s of seq names an owner o with s + o - h divisible by 2. The tiles of one index of seq, over the 2 heads of one index of head, name pairwise different owners. Tiles of one head naming the same cluster have different slots.
All inputs are finite; a program needn't handle non-finite values.
Results may differ from a plain program's by a relative error of at most 0.017.
Values may be sent and summed in bfloat16 or wider, within the bound.
A program may use at most 128 MiB of HBM per device.

v0:
```python
import jax
import jax.numpy as jnp
from jax import lax
from jax.sharding import PartitionSpec as P

CAP = 2


LOGIT_SCALE = 8.0
KEEP_RATE = 0.75


def unit_rows(values, epsilon):
    return values * lax.rsqrt(jnp.mean(values * values, axis=-1, keepdims=True) + epsilon)


def update_centroids(centroid_rows, key_float, token_live, tiles_held, tile_rows):
    key_sums = jnp.sum(key_float * token_live[:, :, None], axis=1)
    counts = tiles_held * tile_rows
    means = key_sums / jnp.maximum(counts, 1.0)[:, None]
    return centroid_rows + (1.0 - KEEP_RATE) * jnp.where(
        counts[:, None] > 0, means - centroid_rows, 0.0
    )


def on_device(tokens, qkv_weight, out_weight, centroids, clusters, slots):
    tok_rows, model_width = tokens.shape
    heads_here, tiles_here = clusters.shape
    clus_here = centroids.shape[1]
    head_dim = centroids.shape[2]
    tile_rows = tok_rows // tiles_here
    seq_count = lax.axis_size("seq")
    normed = unit_rows(tokens.astype(jnp.float32), 1e-05).astype(jnp.bfloat16)
    columns = normed
    projected = jnp.dot(
        columns,
        lax.all_gather(qkv_weight, "seq", axis=0, tiled=True),
        preferred_element_type=jnp.float32,
    ).astype(jnp.bfloat16)
    item_width = tile_rows * 3 * head_dim
    tile_items = (
        projected.reshape(tiles_here, tile_rows, heads_here, 3 * head_dim)
        .transpose(2, 0, 1, 3)
        .reshape(heads_here * tiles_here, item_width)
    )
    owners = (clusters // clus_here).reshape(-1)
    targets = (owners[None, :] == jnp.arange(seq_count, dtype=jnp.int32)[:, None]).astype(jnp.int32)
    outgoing = jnp.dot(
        targets.astype(jnp.bfloat16), tile_items, preferred_element_type=jnp.float32
    ).astype(jnp.bfloat16)
    slot_labels = (
        jnp.arange(heads_here, dtype=jnp.int32)[:, None] * clus_here * CAP
        + clusters % clus_here * CAP
        + slots
    ).reshape(-1) + 1
    tile_labels = jnp.broadcast_to(
        lax.axis_index("seq") * tiles_here + jnp.arange(tiles_here, dtype=jnp.int32),
        (heads_here, tiles_here),
    ).reshape(-1)
    labels = jnp.stack(
        [
            jnp.sum(targets * slot_labels[None, :], axis=1),
            jnp.sum(targets * tile_labels[None, :], axis=1),
        ],
        axis=1,
    )
    incoming, arrived = (
        lax.all_to_all(outgoing, "seq", split_axis=0, concat_axis=0, tiled=True),
        lax.all_to_all(labels, "seq", split_axis=0, concat_axis=0, tiled=True),
    )
    total_slots = heads_here * clus_here * CAP
    placing = (arrived[None, :, 0] - 1 == jnp.arange(total_slots, dtype=jnp.int32)[:, None]).astype(
        jnp.int32
    )
    slotted = jnp.dot(
        placing.astype(jnp.bfloat16), incoming, preferred_element_type=jnp.float32
    ).astype(jnp.bfloat16)
    occupied = jnp.sum(placing, axis=1).astype(jnp.float32)
    tile_of = jnp.sum(placing * arrived[None, :, 1], axis=1)
    batches = heads_here * clus_here
    span_rows = CAP * tile_rows
    cluster_grouped_rows = slotted.reshape(batches, span_rows, 3, head_dim)
    token_live = jnp.repeat(occupied.reshape(batches, CAP), tile_rows, axis=1)
    position = (
        tile_of.reshape(batches, CAP, 1) * tile_rows
        + jnp.arange(tile_rows, dtype=jnp.int32)[None, None, :]
    ).reshape(batches, span_rows)
    normalized_query = unit_rows(cluster_grouped_rows[:, :, 0].astype(jnp.float32), 1e-06).astype(
        jnp.bfloat16
    )
    key_float = unit_rows(cluster_grouped_rows[:, :, 1].astype(jnp.float32), 1e-06)
    normalized_key = key_float.astype(jnp.bfloat16)
    attention_logits = (
        LOGIT_SCALE
        / head_dim
        * jnp.einsum(
            "tra,tla->trl", normalized_query, normalized_key, preferred_element_type=jnp.float32
        )
    )
    diagonal = jnp.arange(span_rows)[:, None] == jnp.arange(span_rows)[None, :]
    allowed = (token_live[:, None, :] > 0) & (
        position[:, None, :] <= position[:, :, None]
    ) | diagonal[None]
    exp_scores = jnp.where(allowed, jnp.exp(attention_logits), 0.0)
    attention_probs = (exp_scores / jnp.sum(exp_scores, axis=-1, keepdims=True)).astype(
        jnp.bfloat16
    )
    attended = jnp.einsum(
        "xjs,xsv->xjv",
        attention_probs,
        cluster_grouped_rows[:, :, 2],
        preferred_element_type=jnp.float32,
    ).astype(jnp.bfloat16)
    tiles_held = jnp.sum(occupied.reshape(batches, CAP), axis=1)
    new_centroids = update_centroids(
        centroids.reshape(batches, head_dim), key_float, token_live, tiles_held, tile_rows
    ).reshape(centroids.shape)
    returning = jnp.dot(
        placing.T.astype(jnp.bfloat16),
        attended.reshape(total_slots, tile_rows * head_dim),
        preferred_element_type=jnp.float32,
    ).astype(jnp.bfloat16)
    answered = lax.all_to_all(returning, "seq", split_axis=0, concat_axis=0, tiled=True)
    returned_rows = jnp.dot(
        targets.T.astype(jnp.bfloat16), answered, preferred_element_type=jnp.float32
    ).astype(jnp.bfloat16)
    attention = (
        returned_rows.reshape(heads_here, tiles_here, tile_rows, head_dim)
        .transpose(1, 2, 0, 3)
        .reshape(tok_rows, heads_here * head_dim)
    )
    full_weight = lax.all_gather(out_weight, "seq", axis=1, tiled=True)
    columns = full_weight
    summed = lax.psum_scatter(
        lax.dot_general(
            columns, attention, (((0,), (1,)), ((), ())), preferred_element_type=jnp.float32
        ).astype(jnp.bfloat16),
        "head",
        scatter_dimension=0,
        tiled=True,
    )
    return (summed, new_centroids)


def solution(mesh):
    placed = (
        P("seq", None),
        P("seq", "head"),
        P("head", "seq"),
        P("head", "seq", None),
        P("head", "seq"),
        P("head", "seq"),
    )
    return jax.shard_map(
        on_device,
        mesh=mesh,
        in_specs=placed,
        out_specs=(P("head", "seq"), P("head", "seq", None)),
        check_vma=False,
    )
```

profile of v0, /device:TPU:1, one launch (start us, length us, event | category | flops | bytes accessed | tf_op | source)
XLA Modules:
  0.0 325.7 jit_solution(1805364900977579055)
XLA Ops:
  9.7 8.6 %all-to-all-start = ((s32[32,1,2]{2,1,0:T(1,128)}), s32[32,1,2]{2,1,0:T(1,128)S(1)}, u32[]{:S(2)}, u32[]{:S(2)}) async-start(s32[32,1,2]{2,1,0:T(1,128)} %copy.36), calls=%async_computation | async-start | bytes 32768 | tf_op jit(solution)/shard_map/all_to_all | solution.py:69
  18.3 5.1 %fusion.2 = f32[1024]{0:T(1024)S(1)} fusion(bf16[1024,4096]{1,0:T(8,128)(2,1)} %param.6), kind=kLoop, calls=%fused_computation.8 | loop fusion | flops 12581888 | bytes 8392704 | tf_op jit(solution)/shard_map/reduce_sum | solution.py:14
  23.4 45.5 %all-gather.3.cloned.1.call-done = bf16[4096,768]{1,0:T(8,128)(2,1)} async-done(((bf16[128,768]{1,0:T(8,128)(2,1)}), bf16[4096,768]{1,0:T(8,128)(2,1)}) %all-gather.3.cloned.1.call-update) | async-done | bytes 6291472 | tf_op jit(solution)/shard_map/all_gather | solution.py:37
  68.9 11.1 %fusion.13 = bf16[1024,768]{1,0:T(8,128)(2,1)S(1)} fusion(bf16[4096,768]{1,0:T(8,128)(2,1)} %all-gather.3.cloned.1.call-done, bf16[1024,4096]{1,0:T(8,128)(2,1)} %param.6, f32[1024]{0:T(1024)S(1)} %add_rsqrt_fusion.2), kind=kOutput, calls=%fused_computation.28 | convolution fusion | flops 6455820288 | bytes 16257024 | tf_op jit(solution)/shard_map/dot_general | solution.py:35
  83.3 3.8 %reduce = bf16[32,49152]{1,0:T(8,128)(2,1)} reduce(bf16[32,1,49152]{2,0,1:T(8,128)(2,1)S(1)} %fusion, bf16[]{:T(256)} %broadcast.210), dimensions={1}, to_apply=%copy.39.reduce_sub_computation | reduce | bytes 6291458 | tf_op jit(solution)/shard_map/all_to_all | solution.py:68
  87.1 5.4 %reshape.181 = bf16[32,2,24576]{2,1,0:T(2,128)(2,1)} reshape(bf16[32,49152]{1,0:T(8,128)(2,1)} %reduce) | data formatting | bytes 6291456
  92.5 4.9 %all-to-all-start.1 = ((bf16[32,2,24576]{2,1,0:T(2,128)(2,1)}), bf16[32,2,24576]{2,1,0:T(2,128)(2,1)S(1)}, u32[]{:S(2)}, u32[]{:S(2)}) async-start(bf16[32,2,24576]{2,1,0:T(2,128)(2,1)} %reshape.181), calls=%async_computation.1 | async-start | bytes 6291456 | tf_op jit(solution)/shard_map/all_to_all | solution.py:68
  99.0 38.0 %all-to-all-done.1 = bf16[32,2,24576]{2,1,0:T(2,128)(2,1)S(1)} async-done(((bf16[32,2,24576]{2,1,0:T(2,128)(2,1)}), bf16[32,2,24576]{2,1,0:T(2,128)(2,1)S(1)}, u32[]{:S(2)}, u32[]{:S(2)}) %all-to-all-start.1) | async-done | bytes 3145760 | tf_op jit(solution)/shard_map/all_to_all | solution.py:68
  137.0 12.4 %reshape.182 = bf16[32,1,49152]{2,1,0:T(2,128)(2,1)} reshape(bf16[32,2,24576]{2,1,0:T(2,128)(2,1)S(1)} %all-to-all-done.1) | data formatting | bytes 6291456
  149.4 7.2 %convolution_convert_fusion = bf16[32,49152]{1,0:T(8,128)(2,1)S(1)} fusion(bf16[32,1,49152]{2,1,0:T(2,128)(2,1)} %reshape.182, s32[32]{0:T(128)S(1)} %get-tuple-element.20), kind=kOutput, calls=%fused_computation | convolution fusion | flops 102239232 | bytes 6291584 | tf_op jit(solution)/shard_map/dot_general | solution.py:75
  156.5 5.5 %reshape.175 = bf16[16,256,3,128]{3,2,1,0:T(4,128)(2,1)} reshape(bf16[32,49152]{1,0:T(8,128)(2,1)S(1)} %convolution_convert_fusion) | data formatting | bytes 6291456 | tf_op jit(solution)/shard_map/reshape | solution.py:82
  162.0 9.6 %fusion.36 = (bf16[16,256,1,128]{3,2,1,0:T(2,128)(2,1)S(1)}, f32[16,256,1,128]{3,2,1,0:T(1,128)S(1)}, f32[16,256,1,128]{3,2,1,0:T(1,128)S(1)}) fusion(bf16[16,256,3,128]{3,2,1,0:T(4,128)(2,1)} %reshape.175), kind=kLoop, calls=%fused_computation.88 | loop fusion | flops 1048576 | bytes 8388608 | tf_op jit(solution)/shard_map/slice | solution.py:111
  172.9 2.4 fusion.9
  175.3 3.2 fusion.16
  178.5 1.3 reshape.176
  179.8 1.7 fusion.1
  181.5 2.1 reduce.1
  183.6 2.6 reshape.183
  186.2 24.1 %all_to_all.36 = bf16[32,2,8192]{2,1,0:T(2,128)(2,1)S(1)} all-to-all(bf16[32,2,8192]{2,1,0:T(2,128)(2,1)} %reshape.183), channel_id=1, replica_groups=mesh['head'=8,'seq'=32] {'seq'}, dimensions={0} | all-to-all | bytes 2097152 | tf_op jit(solution)/shard_map/all_to_all | solution.py:123
  210.3 3.5 %reshape.184 = bf16[32,1,16384]{2,1,0:T(2,128)(2,1)} reshape(bf16[32,2,8192]{2,1,0:T(2,128)(2,1)S(1)} %all_to_all.36) | data formatting | bytes 2097152
  213.8 2.8 fusion.17
  217.1 7.2 %convert_bitcast_fusion = bf16[4096,1024]{0,1:T(8,128)(2,1)} fusion(bf16[256,4096]{1,0:T(8,128)(2,1)} %all-gather.5.cloned.1.call-done, bf16[32,8,8,128]{3,2,1,0:T(8,128)(2,1)S(1)} %bitcast.74), kind=kOutput, calls=%fused_computation.11 | convolution fusion | flops 2151677952 | bytes 11010048 | tf_op jit(solution)/shard_map/dot_general | solution.py:135
  226.5 90.3 %reduce-scatter.2.cloned.1.call-done = bf16[512,1024]{0,1:T(8,128)(2,1)} async-done(((bf16[4096,1024]{0,1:T(8,128)(2,1)}), bf16[512,1024]{0,1:T(8,128)(2,1)}) %reduce-scatter.2.cloned.1.call-update) | async-done | bytes 1048592 | tf_op jit(solution)/shard_map/reduce_scatter | solution.py:134
  316.9 2.3 copy.44
  (51 shorter events, 11.2 us)
Async XLA Ops:
  7.2 61.8 %all-gather.3.cloned.1.call-start = ((), (), s32[]{:S(2)}) async-start(), calls=%async_computation.4 | async-start | bytes 6488064 | tf_op jit(solution)/shard_map/all_gather | solution.py:37
  9.7 82.8 %all-to-all-start = ((s32[32,1,2]{2,1,0:T(1,128)}), s32[32,1,2]{2,1,0:T(1,128)S(1)}, u32[]{:S(2)}, u32[]{:S(2)}) async-start(s32[32,1,2]{2,1,0:T(1,128)} %copy.36), calls=%async_computation | async-start | bytes 32768 | tf_op jit(solution)/shard_map/all_to_all | solution.py:69
  92.5 44.5 %all-to-all-start.1 = ((bf16[32,2,24576]{2,1,0:T(2,128)(2,1)}), bf16[32,2,24576]{2,1,0:T(2,128)(2,1)S(1)}, u32[]{:S(2)}, u32[]{:S(2)}) async-start(bf16[32,2,24576]{2,1,0:T(2,128)(2,1)} %reshape.181), calls=%async_computation.1 | async-start | bytes 6291456 | tf_op jit(solution)/shard_map/all_to_all | solution.py:68
  97.4 119.7 %all-gather.5.cloned.1.call-start = ((), (), s32[]{:S(2)}) async-start(), calls=%async_computation.5 | async-start | bytes 2162688 | tf_op jit(solution)/shard_map/all_gather | solution.py:132
  98.1 218.8 %reduce-scatter.2.cloned.1.call-start = ((), (), s32[]{:S(2)}) async-start(), calls=%async_computation.6 | async-start | bytes 9437184 | tf_op jit(solution)/shard_map/reduce_scatter | solution.py:134
  224.3 1.6 copy-start
Sparse Core Ops, SparseCore 0:
  10.5 58.3 all-gather.2
  100.7 61.9 all-gather.4
  224.4 92.4 reduce-scatter.1
where the time goes:
time: 326 us
  waiting for transfers between devices  175 us (54%)
  local copies, waits for them, and re-layouts  37 us (11%)
  matrix products  36.7 us (11%)
  other arithmetic  24.9 us (8%)
  blocking collectives  24.1 us (7%)
  between operations  14 us (4%)
  starting transfers between devices  13.7 us (4%)
    reduce_scatter x1, waiting for transfers between devices, on_device(): lax.psum_scatter(lax.dot_general(columns, attention, (((0,), (1,)), ((),...  90.3 us
    all_gather x1, waiting for transfers between devices, on_device(): lax.all_gather(qkv_weight, 'seq', axis=0, tiled=True)  45.5 us
    all_to_all x1, waiting for transfers between devices, on_device(): lax.all_to_all(outgoing, 'seq', split_axis=0, concat_axis=0, tiled=True)  38 us
    unnamed x9, local copies, waits for them, and re-layouts  27.1 us
    all_to_all x1, blocking collectives, on_device(): lax.all_to_all(returning, 'seq', split_axis=0, concat_axis=0, tiled=True)  24.1 us
    dot_general x1, matrix products, on_device(): jnp.dot(columns, lax.all_gather(qkv_weight, 'seq', axis=0, tiled=True), p...  11.1 us
    slice x1, other arithmetic, on_device(): cluster_grouped_rows[:, :, 2]  9.61 us
    all_to_all x1, starting transfers between devices, on_device(): lax.all_to_all(labels, 'seq', split_axis=0, concat_axis=0, tiled=True)  8.59 us
  transfers between devices with their start and end apart: 5, of which 3 were waited for; matrix products, arithmetic and copies ran while one was open for 27% of the time, Pallas kernels for 0%

commit v1 on v0

v1 whole, which is shorter than its diff:
```python
import functools

import jax
import jax.numpy as jnp
from jax import lax
from jax.experimental import pallas as pl
from jax.experimental.pallas import tpu as pltpu
from jax.sharding import PartitionSpec as P

MESH = pl.DeviceIdType.MESH
F32 = jnp.float32
BF16 = jnp.bfloat16

NX = 4
NZ = 8
NCHIP = 16
NSEQ = 32
TILE = 128
TILES = 8
HW = 128
QKV = 3 * HW
WROWS = 128
OROWS = 64
OCOLS = 512
LOG2E = 1.4426950408889634
LOGIT = 8.0 / 128


def kernel(
    codes_ref, tok_hbm, w_ref, wo_ref, cent_ref,
    out_ref, newc_ref,
    tok, wbuf, obuf, owt, rscale,
    qkv0, qkv1, stage0, stage1, recv0, recv1, ret0, ret1, back0, back1,
    gbuf, acc, ksum,
    t_inv, t_lab, t_tile, t_par, t_lim, t_dst,
    tok_sem, w_send, w_recv, o_send, o_recv, sc_send, sc_recv, loc_sem,
    a_send, a_recv, r_send, r_recv, z_send, z_recv,
):
    z = lax.axis_index("head")
    s = lax.axis_index("seq")
    c = s % 2
    q = s // 2
    x = q % NX
    y = q // NX
    u = y * (1 - c) + x * c
    v = x * (1 - c) + y * c
    qkv = (qkv0, qkv1)
    stage = (stage0, stage1)
    recv = (recv0, recv1)
    ret = (ret0, ret1)
    back = (back0, back1)

    for t in range(TILES):
        pltpu.make_async_copy(
            tok_hbm.at[pl.ds(t * TILE, TILE)], tok.at[pl.ds(t * TILE, TILE)], tok_sem.at[t]
        ).start()
    own_w = pl.ds(pl.multiple_of(s * WROWS, WROWS), WROWS)
    wbuf[own_w, :] = w_ref[...]

    zg = s // 4
    barrier = pltpu.get_barrier_semaphore()

    def greet(i, carry):
        pl.semaphore_signal(barrier, inc=1, device_id=(z, (s + i) % NSEQ), device_id_type=MESH)
        return carry

    lax.fori_loop(1, NSEQ, greet, 0)
    pl.semaphore_signal(barrier, inc=1, device_id=((z + 1) % NZ, s), device_id_type=MESH)
    pl.semaphore_signal(barrier, inc=1, device_id=((z + NZ - 1) % NZ, s), device_id_type=MESH)

    @pl.when(zg != z)
    def _():
        for i in range(4):
            pl.semaphore_signal(barrier, inc=1, device_id=(zg, 4 * z + i), device_id_type=MESH)

    pl.semaphore_wait(barrier, jnp.where(zg != z, NSEQ - 1 + 2 + 4, NSEQ - 1 + 2))

    def slot(cc, uu, vv):
        uu = uu % NX
        vv = vv % NX
        yy = uu * (1 - cc) + vv * cc
        xx = vv * (1 - cc) + uu * cc
        return (yy * NX + xx) * 2 + cc

    class Gather:
        def __init__(self, buf, rows, send, recv_sem):
            self.buf, self.rows, self.send, self.recv = buf, rows, send, recv_sem

        def copy(self, sl, part, dev, sem):
            rows = self.rows
            if part is None:
                ref = self.buf.at[pl.ds(pl.multiple_of(sl * rows, rows), rows)]
            else:
                half = rows // 2
                ref = self.buf.at[pl.ds(pl.multiple_of(sl * rows + part * half, half), half)]
            return pltpu.make_async_remote_copy(
                src_ref=ref, dst_ref=ref, send_sem=self.send.at[sem], recv_sem=self.recv.at[sem],
                device_id=(z, dev), device_id_type=MESH,
            )

        def v_copy(self, k, recv_side=False):
            if k == 0:
                sl = slot(c, u, v - 1 if recv_side else v)
                return self.copy(sl, None, slot(c, u, v + 1), 0)
            if k == 1:
                sl = slot(c, u, v + 1 if recv_side else v)
                return self.copy(sl, None, slot(c, u, v - 1), 1)
            if k == 2:
                sl = slot(c, u, v - 2 if recv_side else v - 1)
                return self.copy(sl, 0, slot(c, u, v + 1), 2)
            sl = slot(c, u, v + 2 if recv_side else v + 1)
            return self.copy(sl, 1, slot(c, u, v - 1), 3)

        def u_copy(self, j, k, recv_side=False):
            vv = v + (0, -1, 1, 2)[j]
            sem = 4 + 4 * j + k
            if k == 0:
                sl = slot(c, u - 1 if recv_side else u, vv)
                return self.copy(sl, None, slot(c, u + 1, v), sem)
            if k == 1:
                sl = slot(c, u + 1 if recv_side else u, vv)
                return self.copy(sl, None, slot(c, u - 1, v), sem)
            if k == 2:
                sl = slot(c, u - 2 if recv_side else u - 1, vv)
                return self.copy(sl, 0, slot(c, u + 1, v), sem)
            sl = slot(c, u + 2 if recv_side else u + 1, vv)
            return self.copy(sl, 1, slot(c, u - 1, v), sem)

        def c_copy(self, a, j, recv_side=False):
            du = (0, -1, 1, 2)[a]
            dv = (0, -1, 1, 2)[j]
            if recv_side:
                sl = slot(1 - c, v + du, u + dv)
            else:
                sl = slot(c, u + du, v + dv)
            return self.copy(sl, None, s + 1 - 2 * c, 20 + 4 * a + j)

        def steps(self):
            def first():
                self.v_copy(0).start()
                self.v_copy(1).start()
                self.u_copy(0, 0).start()
                self.u_copy(0, 1).start()
                self.c_copy(0, 0).start()

            def second():
                self.v_copy(0, True).wait_recv()
                self.v_copy(2).start()
                self.v_copy(1, True).wait_recv()
                self.v_copy(3).start()
                for j in (1, 2):
                    self.u_copy(j, 0).start()
                    self.u_copy(j, 1).start()
                    self.c_copy(0, j).start()

            def third():
                self.v_copy(2, True).wait_recv()
                self.v_copy(3, True).wait_recv()
                self.u_copy(3, 0).start()
                self.u_copy(3, 1).start()
                self.c_copy(0, 3).start()

            def along(j):
                def run():
                    self.u_copy(j, 0, True).wait_recv()
                    self.u_copy(j, 2).start()
                    self.c_copy(1, j).start()
                    self.u_copy(j, 1, True).wait_recv()
                    self.u_copy(j, 3).start()
                    self.c_copy(2, j).start()
                return run

            def far(j):
                def run():
                    self.u_copy(j, 2, True).wait_recv()
                    self.u_copy(j, 3, True).wait_recv()
                    self.c_copy(3, j).start()
                return run

            def last():
                for a in range(4):
                    for j in range(4):
                        self.c_copy(a, j, True).wait_recv()

            return [
                first, second, along(0), third, along(1), along(2), far(0), along(3),
                far(1), far(2), far(3), last,
            ]

        def drain(self):
            for k in range(4):
                self.v_copy(k).wait_send()
            for j in range(4):
                for k in range(4):
                    self.u_copy(j, k).wait_send()
            for a in range(4):
                for j in range(4):
                    self.c_copy(a, j).wait_send()

    gather_w = Gather(wbuf, WROWS, w_send, w_recv)
    gather_o = Gather(obuf, OROWS, o_send, o_recv)
    w_steps = gather_w.steps()
    o_steps = gather_o.steps()
    w_steps[0]()

    own_o = pl.multiple_of(s * OROWS, OROWS)

    def scatter(i):
        return pltpu.make_async_remote_copy(
            src_ref=wo_ref.at[pl.ds(i * OROWS, OROWS)],
            dst_ref=obuf.at[pl.ds(pl.multiple_of((4 * z + i) * OROWS, OROWS), OROWS),
                            pl.ds(pl.multiple_of((s % 4) * 128, 128), 128)],
            send_sem=sc_send.at[i], recv_sem=sc_recv.at[s % 4],
            device_id=(zg, 4 * z + i), device_id_type=MESH,
        )

    def scattered(j):
        return pltpu.make_async_remote_copy(
            src_ref=wo_ref.at[pl.ds(j * OROWS, OROWS)],
            dst_ref=obuf.at[pl.ds(own_o, OROWS), pl.ds(j * 128, 128)],
            send_sem=sc_send.at[j], recv_sem=sc_recv.at[j],
            device_id=(zg, 4 * z + j), device_id_type=MESH,
        )

    for i in range(4):
        is_self = (zg == z) & (s % 4 == i)

        @pl.when(jnp.logical_not(is_self))
        def _(i=i):
            scatter(i).start()

        @pl.when(is_self)
        def _(i=i):
            cp = pltpu.make_async_copy(
                wo_ref.at[pl.ds(i * OROWS, OROWS)],
                obuf.at[pl.ds(own_o, OROWS), pl.ds(i * 128, 128)],
                loc_sem,
            )
            cp.start()
            cp.wait()

    def scales(t):
        pltpu.make_async_copy(
            tok_hbm.at[pl.ds(t * TILE, TILE)], tok.at[pl.ds(t * TILE, TILE)], tok_sem.at[t]
        ).wait()

        def rows(i, carry):
            at = pl.ds(pl.multiple_of(t * TILE + i * 16, 16), 16)
            val = tok[at, :].astype(F32)
            mean = jnp.sum(val * val, axis=-1, keepdims=True) * (1.0 / tok.shape[1])
            rscale[at, :] = jnp.broadcast_to(lax.rsqrt(mean + 1e-5), (16, 128))
            return carry

        lax.fori_loop(0, TILE // 16, rows, 0)

    def tables(h):
        def per_offset(d, carry):
            dy, dx = d // NX, d % NX
            src = (((y + NX - dy) % NX) * NX + (x + NX - dx) % NX) * 2 + (c + h) % 2
            dst = (((y + dy) % NX) * NX + (x + dx) % NX) * 2 + (c + h) % 2
            lab = jnp.int32(-1)
            til = jnp.int32(0)
            inv = jnp.int32(0)
            for t in range(TILES):
                code = codes_ref[src, h * TILES + t]
                hit = (code // 16) == s
                lab = jnp.where(hit, code % 16, lab)
                til = jnp.where(hit, t, til)
                mine = codes_ref[s, h * TILES + t]
                inv = jnp.where((mine // 16) == dst, t, inv)
            t_lab[h, d] = lab
            t_tile[h, d] = src * TILES + til
            t_inv[h, d] = inv
            return carry

        lax.fori_loop(0, NCHIP, per_offset, 0)

        def per_arrival(d, carry):
            lab = t_lab[h, d]
            want = jnp.where(lab < 0, -2, lab + 1 - 2 * (lab % 2))
            til = t_tile[h, d]
            par = d
            lim = jnp.int32(TILE)
            for e in range(NCHIP):
                hit = t_lab[h, e] == want
                par = jnp.where(hit, e, par)
                lim = jnp.where(hit & (t_tile[h, e] < til), 2 * TILE, lim)
            t_par[h, d] = par
            t_lim[h, d] = lim
            return carry

        lax.fori_loop(0, NCHIP, per_arrival, 0)
        for t in range(TILES):
            owner = codes_ref[s, h * TILES + t] // 32
            oy, ox = owner // NX, owner % NX
            t_dst[h, t] = ((oy + NX - y) % NX) * NX + (ox + NX - x) % NX

    work = [functools.partial(scales, t) for t in range(TILES)]
    work += [functools.partial(tables, h) for h in range(2)]
    order = list(w_steps[1:])
    while order or work:
        if work:
            work.pop(0)()
        if order and (len(order) > 1 or not work):
            order.pop(0)()

    def project(h):
        def rows(m, carry):
            at = pl.ds(pl.multiple_of(m * 256, 256), 256)
            val = jnp.dot(tok[at, :], wbuf[:, h * QKV:(h + 1) * QKV], preferred_element_type=F32)
            rs = rscale[at, :]
            parts = []
            for p in range(3):
                vp = (val[:, p * HW:(p + 1) * HW] * rs).astype(BF16)
                if p < 2:
                    vf = vp.astype(F32)
                    mean = jnp.mean(vf * vf, axis=-1, keepdims=True)
                    unit = vf * lax.rsqrt(mean + 1e-6)
                    if p == 0:
                        unit = unit * (LOGIT * LOG2E)
                    vp = unit.astype(BF16)
                parts.append(vp)
            whole = jnp.concatenate(parts, axis=1)
            qkv[h][pl.ds(m * 2, 2)] = whole.reshape(2, TILE, QKV)
            return carry

        lax.fori_loop(0, TILES // 2, rows, 0)

    def a_copy(h, d, recv_side=False):
        dy, dx = d // NX, d % NX
        dev = (((y + dy) % NX) * NX + (x + dx) % NX) * 2 + (c + h) % 2
        return pltpu.make_async_remote_copy(
            src_ref=stage[h].at[d], dst_ref=recv[h].at[d],
            send_sem=a_send.at[h, d], recv_sem=a_recv.at[h, d],
            device_id=(z, dev), device_id_type=MESH,
        )

    def r_copy(h, d):
        dy, dx = d // NX, d % NX
        dev = (((y + NX - dy) % NX) * NX + (x + NX - dx) % NX) * 2 + (c + h) % 2
        return pltpu.make_async_remote_copy(
            src_ref=ret[h].at[d], dst_ref=back[h].at[d],
            send_sem=r_send.at[h, d], recv_sem=r_recv.at[h, d],
            device_id=(z, dev), device_id_type=MESH,
        )

    def send_tiles(h):
        if h == 0:
            recv[0][0] = qkv[0][t_inv[0, 0]]

        def one(d, carry):
            stage[h][d] = qkv[h][t_inv[h, d]]
            a_copy(h, d).start()
            return carry

        lax.fori_loop(1 - h, NCHIP, one, 0)

    def arrivals(h):
        def one(d, carry):
            a_copy(h, d).wait_recv()
            return carry

        lax.fori_loop(1 - h, NCHIP, one, 0)

    def attend(h):
        row = lax.broadcasted_iota(jnp.int32, (TILE, 2 * TILE), 0)
        col = lax.broadcasted_iota(jnp.int32, (TILE, 2 * TILE), 1)
        ones = jnp.ones((2 * TILE, HW), BF16)

        def one(d, store):
            par = t_par[h, d]
            lim = t_lim[h, d]
            mine = recv[h][d]
            other = recv[h][par]
            keys = jnp.concatenate([mine[:, HW:2 * HW], other[:, HW:2 * HW]], axis=0)
            vals = jnp.concatenate([mine[:, 2 * HW:], other[:, 2 * HW:]], axis=0)
            logits = lax.dot_general(
                mine[:, :HW], keys, (((1,), (1,)), ((), ())), preferred_element_type=F32
            )
            allowed = (col <= row) | ((col >= TILE) & (col < lim))
            probs = jnp.where(allowed, jnp.exp2(logits), 0.0).astype(BF16)
            both = jnp.dot(
                probs, jnp.concatenate([vals, ones], axis=1), preferred_element_type=F32
            )
            store[h][d] = (both[:, :HW] / both[:, HW:]).astype(BF16)
            ksum[h, d] = jnp.sum(mine[:, HW:2 * HW].astype(F32).reshape(16, 8, HW), axis=0)

        if h == 0:
            one(0, back)

        def loop(d, carry):
            one(d, ret)
            r_copy(h, d).start()
            return carry

        lax.fori_loop(1 - h, NCHIP, loop, 0)

    def centroids(h):
        rows8 = lax.broadcasted_iota(jnp.int32, (8, HW), 0)

        def one(d, carry):
            sums, counts = carry
            cl = (t_lab[h, d] + 2) // 2 - 1
            hit = rows8 == cl
            tot = jnp.sum(ksum[h, d], axis=0, keepdims=True)
            sums = sums + jnp.where(hit, jnp.broadcast_to(tot, (8, HW)), 0.0)
            counts = counts + jnp.where(hit, float(TILE), 0.0)
            return sums, counts

        zero = jnp.zeros((8, HW), F32)
        sums, counts = lax.fori_loop(0, NCHIP, one, (zero, zero))
        cent = cent_ref[h]
        means = sums / jnp.maximum(counts, 1.0)
        newc_ref[h] = cent + 0.25 * jnp.where(counts > 0, means - cent, 0.0)

    def come_home(h):
        def one(d, carry):
            r_copy(h, d).wait_recv()
            return carry

        lax.fori_loop(1 - h, NCHIP, one, 0)
        for t in range(TILES):
            gbuf[h, z, pl.ds(t * TILE, TILE)] = back[h][t_dst[h, t]]

    half = TILES * TILE // 2

    def z_copy(h, way, k, j, recv_side=False):
        sign = 1 if way == 0 else -1
        at = z - sign * (k - 1)
        if recv_side:
            at = at - sign
        ref = gbuf.at[h, (at + 2 * NZ) % NZ, pl.ds(j * half, half)]
        idx = way * 8 + (k - 1) * 2 + j
        return pltpu.make_async_remote_copy(
            src_ref=ref, dst_ref=ref, send_sem=z_send.at[h, idx], recv_sem=z_recv.at[h, idx],
            device_id=((z + sign + NZ) % NZ, s), device_id_type=MESH,
        )

    def z_parts(k):
        if k < 4:
            return [(way, j) for j in range(2) for way in range(2)]
        return [(0, 0), (1, 1)]

    def z_first(h):
        for way, j in z_parts(1):
            z_copy(h, way, 1, j).start()

    def z_step(h, k):
        nxt = z_parts(k + 1) if k < 4 else []
        for way, j in z_parts(k):
            z_copy(h, way, k, j, True).wait_recv()
            if (way, j) in nxt:
                z_copy(h, way, k + 1, j).start()

    def z_drain(h):
        for k in range(1, 5):
            for way, j in z_parts(k):
                z_copy(h, way, k, j).wait_send()

    def multiply(h, ga, gb, mode):
        ga = (z + ga) % NZ
        gb = (z + gb) % NZ

        def cols(n, carry):
            at = pl.ds(pl.multiple_of(n * 256, 256), 256)
            rhs = jnp.concatenate([gbuf[h, ga, at], gbuf[h, gb, at]], axis=1)
            lhs = jnp.concatenate([owt[h, ga], owt[h, gb]], axis=1)
            val = lax.dot_general(lhs, rhs, (((1,), (1,)), ((), ())), preferred_element_type=F32)
            if mode != "first":
                val = val + acc[n]
            if mode == "last":
                for m in range(4):
                    @pl.when(n == m)
                    def _(m=m):
                        out_ref[:, m * 256:(m + 1) * 256] = val.astype(BF16)
            else:
                acc[n] = val
            return carry

        lax.fori_loop(0, 4, cols, 0)

    project(0)
    send_tiles(0)
    project(1)
    send_tiles(1)
    arrivals(0)
    attend(0)
    come_home(0)
    z_first(0)
    arrivals(1)
    z_step(0, 1)
    attend(1)
    centroids(0)
    for j in range(4):
        not_self = (zg != z) | (s % 4 != j)

        @pl.when(not_self)
        def _(j=j):
            scattered(j).wait_recv()

    o_steps[0]()
    z_step(0, 2)
    o_steps[1]()
    come_home(1)
    z_first(1)
    centroids(1)
    z_step(0, 3)
    for f in o_steps[2:]:
        f()
    for g in range(NZ):
        for h in range(2):
            at = (g * 2 + h) * HW
            owt[h, g] = obuf[at:at + HW, :].astype(F32).T.astype(BF16)
    z_step(1, 1)
    z_step(0, 4)
    multiply(0, 0, 1, "first")
    multiply(0, 7, 2, "mid")
    z_step(1, 2)
    multiply(0, 6, 3, "mid")
    multiply(0, 5, 4, "mid")
    multiply(1, 1, 7, "mid")
    z_step(1, 3)
    multiply(1, 2, 6, "mid")
    multiply(1, 3, 5, "mid")
    z_step(1, 4)
    multiply(1, 0, 4, "last")

    gather_w.drain()
    gather_o.drain()
    for i in range(4):
        @pl.when((zg != z) | (s % 4 != i))
        def _(i=i):
            scatter(i).wait_send()

    for h in range(2):
        def sent(d, carry, h=h):
            a_copy(h, d).wait_send()
            r_copy(h, d).wait_send()
            return carry

        lax.fori_loop(1 - h, NCHIP, sent, 0)
        z_drain(h)


def on_device(tokens, qkv_weight, out_weight, centroids, clusters, slots):
    codes = lax.all_gather(clusters * 2 + slots, "seq", axis=0, tiled=False).reshape(NSEQ, 16)
    vmem = pl.BlockSpec(memory_space=pltpu.VMEM)
    dma = pltpu.SemaphoreType.DMA
    return pl.pallas_call(
        kernel,
        out_shape=(
            jax.ShapeDtypeStruct((OCOLS, TILES * TILE), BF16),
            jax.ShapeDtypeStruct(centroids.shape, F32),
        ),
        in_specs=[
            pl.BlockSpec(memory_space=pltpu.SMEM),
            pl.BlockSpec(memory_space=pl.ANY),
            vmem, vmem, vmem,
        ],
        out_specs=(vmem, vmem),
        scratch_shapes=[
            pltpu.VMEM(tokens.shape, BF16),
            pltpu.VMEM((NSEQ * WROWS, 2 * QKV), BF16),
            pltpu.VMEM((NSEQ * OROWS, OCOLS), BF16),
            pltpu.VMEM((2, NZ, OCOLS, HW), BF16),
            pltpu.VMEM((TILES * TILE, 128), F32),
        ]
        + [pltpu.VMEM((TILES, TILE, QKV), BF16)] * 2
        + [pltpu.VMEM((NCHIP, TILE, QKV), BF16)] * 4
        + [pltpu.VMEM((NCHIP, TILE, HW), BF16)] * 4
        + [
            pltpu.VMEM((2, NZ, TILES * TILE, HW), BF16),
            pltpu.VMEM((4, OCOLS, 256), F32),
            pltpu.VMEM((2, NCHIP, 8, HW), F32),
        ]
        + [pltpu.SMEM((2, NCHIP), jnp.int32)] * 5
        + [pltpu.SMEM((2, TILES), jnp.int32)]
        + [
            dma((TILES,)), dma((36,)), dma((36,)), dma((36,)), dma((36,)),
            dma((4,)), dma((4,)), dma,
            dma((2, NCHIP)), dma((2, NCHIP)), dma((2, NCHIP)), dma((2, NCHIP)),
            dma((2, 16)), dma((2, 16)),
        ],
        compiler_params=pltpu.CompilerParams(
            collective_id=0, has_side_effects=True, vmem_limit_bytes=60 * 1024 * 1024
        ),
    )(codes, tokens, qkv_weight, out_weight, centroids)


def solution(mesh):
    return jax.shard_map(
        on_device,
        mesh=mesh,
        in_specs=(
            P("seq", None),
            P("seq", "head"),
            P("head", "seq"),
            P("head", "seq", None),
            P("head", "seq"),
            P("head", "seq"),
        ),
        out_specs=(P("head", "seq"), P("head", "seq", None)),
        check_vma=False,
    )
```

time: 326 us -> 178 us (0.55)
  waiting for transfers between devices: 175 us -> 0 us
  Pallas kernels: 0 us -> 146 us
  matrix products: 36.7 us -> 0 us
  local copies, waits for them, and re-layouts: 37 us -> 4.32 us
  other arithmetic: 24.9 us -> 0.7 us
  starting transfers between devices: 13.7 us -> 0 us
  between operations: 14 us -> 0.64 us
    pallas_call x0 -> x1, Pallas kernels: none -> 146 us  [on_device(): pl.pallas_call(kernel, out_shape=(jax.ShapeDtypeStruct((OCOLS, TILES * TI...]
    reduce_scatter x1 -> x0, waiting for transfers between devices: 90.3 us -> none  [on_device(): lax.psum_scatter(lax.dot_general(columns, attention, (((0,), (1,)), ((),...]
    all_gather x2 -> x0, waiting for transfers between devices: 45.5 us -> none  [the longest x1 45.5 us: on_device(): lax.all_gather(qkv_weight, 'seq', axis=0, tiled=True)]
    all_to_all x2 -> x0, waiting for transfers between devices: 38 us -> none  [the longest x1 38 us: on_device(): lax.all_to_all(outgoing, 'seq', split_axis=0, concat_axis=0, tiled=True)]
    dot_general x8 -> x0, matrix products: 36.7 us -> none  [the longest x1 11.1 us: on_device(): jnp.dot(columns, lax.all_gather(qkv_weight, 'seq', axis=0, tiled=True), p...]
    all_gather x0 -> x1, blocking collectives: none -> 25.8 us  [on_device(): lax.all_gather(clusters * 2 + slots, 'seq', axis=0, tiled=False)]
    all_to_all x1 -> x0, blocking collectives: 24.1 us -> none  [on_device(): lax.all_to_all(returning, 'seq', split_axis=0, concat_axis=0, tiled=True)]
    unnamed x9 -> x2, local copies, waits for them, and re-layouts: 27.1 us -> 3.56 us
  transfers between devices with their start and end apart: 5 -> 0, of which waited for: 3 -> 0; matrix products, arithmetic and copies ran while one was open for 27% -> 0% of each run, Pallas kernels for 0% -> 0%
where the time goes in v1:
time: 178 us; the launch traced here: 177 us
  Pallas kernels  146 us (82%)
  blocking collectives  25.8 us (14%)
  local copies, waits for them, and re-layouts  4.32 us (2%)
    pallas_call x1, Pallas kernels, on_device(): pl.pallas_call(kernel, out_shape=(jax.ShapeDtypeStruct((OCOLS, TILES * TI...  146 us
    all_gather x1, blocking collectives, on_device(): lax.all_gather(clusters * 2 + slots, 'seq', axis=0, tiled=False)  25.8 us

profile of v1, /device:TPU:1, one launch (start us, length us, event | category | flops | bytes accessed | tf_op | source)
XLA Modules:
  0.0 177.4 jit_solution(12842255258165289967)
XLA Ops:
  0.6 0.7 add_bitcast_fusion
  1.3 25.8 %all-gather.1 = s32[32,2,8]{2,1,0:T(2,128)S(1)} all-gather(s32[1,2,8]{2,1,0:T(2,128)S(1)} %add_bitcast_fusion), channel_id=2, replica_groups=mesh['head'=8,'seq'=32] {'seq'}, dimensions={0}, use_global_device_ids=true | all-gather | bytes 2112 | tf_op jit(solution)/shard_map/all_gather | solution.py:546
  27.1 0.1 copy.10
  27.2 0.7 copy.11.codes_ref
  27.9 146.0 %shard_map.77 = (bf16[512,1024]{1,0:T(8,128)(2,1)}, f32[2,8,128]{2,1,0:T(8,128)}) custom-call(s32[32,16]{1,0:T(8,128)} %copy.11.codes_ref, bf16[1024,4096]{1,0:T(8,128)(2,1)} %tok_hbm.1, bf16[128,768]{1,0:T(8,128)(2,1)} %w_ref.1, bf16[256,128]{1,0:T(8,128)(2,1)} %wo_ref.1, f32[2,8,128]{2,1,0:T(8,128)} %cent_ref.1), custom_call_target="tpu_custom_call" | custom-call | tf_op jit(solution)/shard_map/pallas_call | solution.py:549
  173.9 2.3 %copy.14 = bf16[512,1024]{1,0:T(8,128)(2,1)} copy(bf16[512,1024]{1,0:T(8,128)(2,1)} %get-tuple-element.4) | data formatting | bytes 2097152
  176.1 1.3 copy.15

commit v2 on v1

--- a/solution.py
+++ b/solution.py
@@ -22,19 +22,20 @@
 WROWS = 128
 OROWS = 64
 OCOLS = 512
+MROWS = TILE + 8
 LOG2E = 1.4426950408889634
 LOGIT = 8.0 / 128
 
 
 def kernel(
-    codes_ref, tok_hbm, w_ref, wo_ref, cent_ref,
+    clus_ref, slot_ref, tok_hbm, w_ref, wo_ref, cent_ref,
     out_ref, newc_ref,
     tok, wbuf, obuf, owt, rscale,
     qkv0, qkv1, stage0, stage1, recv0, recv1, ret0, ret1, back0, back1,
-    gbuf, acc, ksum,
-    t_inv, t_lab, t_tile, t_par, t_lim, t_dst,
+    gbuf, acc, msg0, msg1, own0, own1, late,
+    codes_ref, cbuf, t_inv, t_lab, t_tile, t_par, t_lim, t_dst,
     tok_sem, w_send, w_recv, o_send, o_recv, sc_send, sc_recv, loc_sem,
-    a_send, a_recv, r_send, r_recv, z_send, z_recv,
+    a_send, a_recv, r_send, r_recv, z_send, z_recv, m_send, m_recv,
 ):
     z = lax.axis_index("head")
     s = lax.axis_index("seq")
@@ -49,6 +50,8 @@
     recv = (recv0, recv1)
     ret = (ret0, ret1)
     back = (back0, back1)
+    msg = (msg0, msg1)
+    own = (own0, own1)
 
     for t in range(TILES):
         pltpu.make_async_copy(
@@ -56,6 +59,9 @@
         ).start()
     own_w = pl.ds(pl.multiple_of(s * WROWS, WROWS), WROWS)
     wbuf[own_w, :] = w_ref[...]
+    own_codes = clus_ref[...] * 2 + slot_ref[...]
+    cbuf[s] = jnp.full((2, 128), -16, jnp.int32)
+    cbuf[s, :, 0:TILES] = own_codes
 
     zg = s // 4
     barrier = pltpu.get_barrier_semaphore()
@@ -72,6 +78,20 @@
     def _():
         for i in range(4):
             pl.semaphore_signal(barrier, inc=1, device_id=(zg, 4 * z + i), device_id_type=MESH)
+
+    def scales(t):
+        pltpu.make_async_copy(
+            tok_hbm.at[pl.ds(t * TILE, TILE)], tok.at[pl.ds(t * TILE, TILE)], tok_sem.at[t]
+        ).wait()
+
+        def rows(i, carry):
+            at = pl.ds(pl.multiple_of(t * TILE + i * 16, 16), 16)
+            val = tok[at, :].astype(F32)
+            mean = jnp.sum(val * val, axis=-1, keepdims=True) * (1.0 / tok.shape[1])
+            rscale[at, :] = jnp.broadcast_to(lax.rsqrt(mean + 1e-5), (16, 128))
+            return carry
+
+        lax.fori_loop(0, TILE // 16, rows, 0)
 
     pl.semaphore_wait(barrier, jnp.where(zg != z, NSEQ - 1 + 2 + 4, NSEQ - 1 + 2))
 
@@ -83,16 +103,17 @@
         return (yy * NX + xx) * 2 + cc
 
     class Gather:
-        def __init__(self, buf, rows, send, recv_sem):
+        def __init__(self, buf, rows, send, recv_sem, cols=None):
             self.buf, self.rows, self.send, self.recv = buf, rows, send, recv_sem
+            self.cols = slice(None) if cols is None else pl.ds(*cols)
 
         def copy(self, sl, part, dev, sem):
             rows = self.rows
             if part is None:
-                ref = self.buf.at[pl.ds(pl.multiple_of(sl * rows, rows), rows)]
+                ref = self.buf.at[pl.ds(pl.multiple_of(sl * rows, rows), rows), self.cols]
             else:
                 half = rows // 2
-                ref = self.buf.at[pl.ds(pl.multiple_of(sl * rows + part * half, half), half)]
+                ref = self.buf.at[pl.ds(pl.multiple_of(sl * rows + part * half, half), half), self.cols]
             return pltpu.make_async_remote_copy(
                 src_ref=ref, dst_ref=ref, send_sem=self.send.at[sem], recv_sem=self.recv.at[sem],
                 device_id=(z, dev), device_id_type=MESH,
@@ -197,11 +218,51 @@
                 for j in range(4):
                     self.c_copy(a, j).wait_send()
 
-    gather_w = Gather(wbuf, WROWS, w_send, w_recv)
+    gather_w = [
+        Gather(wbuf, WROWS, w_send.at[h], w_recv.at[h], (h * QKV, QKV)) for h in range(2)
+    ]
     gather_o = Gather(obuf, OROWS, o_send, o_recv)
-    w_steps = gather_w.steps()
+    w_steps = [g.steps() for g in gather_w]
     o_steps = gather_o.steps()
-    w_steps[0]()
+    w_steps[0][0]()
+    w_steps[1][0]()
+
+    def code_copy(i, recv_side=False):
+        at = (s + NSEQ - i) % NSEQ if recv_side else s
+        return pltpu.make_async_remote_copy(
+            src_ref=cbuf.at[at], dst_ref=cbuf.at[at], send_sem=m_send.at[i], recv_sem=m_recv.at[i],
+            device_id=(z, (s + i) % NSEQ), device_id_type=MESH,
+        )
+
+    def send_codes(i, carry):
+        code_copy(i).start()
+        return carry
+
+    lax.fori_loop(1, NSEQ, send_codes, 0)
+
+    def codes_here():
+        def one(i, carry):
+            code_copy(i, True).wait_recv()
+            return carry
+
+        lax.fori_loop(1, NSEQ, one, 0)
+        pltpu.make_async_copy(cbuf, codes_ref, loc_sem).start()
+
+    def codes_read():
+        pltpu.make_async_copy(cbuf, codes_ref, loc_sem).wait()
+
+    def lateness():
+        place = lax.broadcasted_iota(jnp.int32, (NSEQ, 128), 0) * TILES
+        place = place + lax.broadcasted_iota(jnp.int32, (NSEQ, 128), 1)
+        for h in range(2):
+            codes = cbuf[:, h, :]
+            for t in range(TILES):
+                mine = own_codes[h:h + 1, t:t + 1]
+                want = jnp.broadcast_to(mine + 1 - 2 * (mine % 2), (NSEQ, 128))
+                hit = (codes == want) & (place < s * TILES + t)
+                some = jnp.max(jnp.where(hit, 1, 0), axis=0, keepdims=True)
+                some = jnp.max(some, axis=1, keepdims=True)
+                late[h * TILES + t:h * TILES + t + 1, :] = jnp.broadcast_to(some, (1, 128))
 
     own_o = pl.multiple_of(s * OROWS, OROWS)
 
@@ -239,20 +300,6 @@
             cp.start()
             cp.wait()
 
-    def scales(t):
-        pltpu.make_async_copy(
-            tok_hbm.at[pl.ds(t * TILE, TILE)], tok.at[pl.ds(t * TILE, TILE)], tok_sem.at[t]
-        ).wait()
-
-        def rows(i, carry):
-            at = pl.ds(pl.multiple_of(t * TILE + i * 16, 16), 16)
-            val = tok[at, :].astype(F32)
-            mean = jnp.sum(val * val, axis=-1, keepdims=True) * (1.0 / tok.shape[1])
-            rscale[at, :] = jnp.broadcast_to(lax.rsqrt(mean + 1e-5), (16, 128))
-            return carry
-
-        lax.fori_loop(0, TILE // 16, rows, 0)
-
     def tables(h):
         def per_offset(d, carry):
             dy, dx = d // NX, d % NX
@@ -262,11 +309,11 @@
             til = jnp.int32(0)
             inv = jnp.int32(0)
             for t in range(TILES):
-                code = codes_ref[src, h * TILES + t]
+                code = codes_ref[src, h, t]
                 hit = (code // 16) == s
                 lab = jnp.where(hit, code % 16, lab)
                 til = jnp.where(hit, t, til)
-                mine = codes_ref[s, h * TILES + t]
+                mine = codes_ref[s, h, t]
                 inv = jnp.where((mine // 16) == dst, t, inv)
             t_lab[h, d] = lab
             t_tile[h, d] = src * TILES + til
@@ -291,40 +338,53 @@
 
         lax.fori_loop(0, NCHIP, per_arrival, 0)
         for t in range(TILES):
-            owner = codes_ref[s, h * TILES + t] // 32
+            owner = codes_ref[s, h, t] // 32
             oy, ox = owner // NX, owner % NX
             t_dst[h, t] = ((oy + NX - y) % NX) * NX + (ox + NX - x) % NX
 
-    work = [functools.partial(scales, t) for t in range(TILES)]
-    work += [functools.partial(tables, h) for h in range(2)]
-    order = list(w_steps[1:])
-    while order or work:
-        if work:
-            work.pop(0)()
-        if order and (len(order) > 1 or not work):
-            order.pop(0)()
-
-    def project(h):
-        def rows(m, carry):
+    lag = 4
+    for k in range(1, 12):
+        w_steps[0][k]()
+        if k <= TILES:
+            scales(k - 1)
+        if k - lag >= 1:
+            w_steps[1][k - lag]()
+        if k == 5:
+            codes_here()
+            lateness()
+        if k == 8:
+            codes_read()
+        if k in (8, 9):
+            tables(k - 8)
+
+    def project(h, m):
+        if True:
             at = pl.ds(pl.multiple_of(m * 256, 256), 256)
             val = jnp.dot(tok[at, :], wbuf[:, h * QKV:(h + 1) * QKV], preferred_element_type=F32)
             rs = rscale[at, :]
-            parts = []
-            for p in range(3):
-                vp = (val[:, p * HW:(p + 1) * HW] * rs).astype(BF16)
-                if p < 2:
-                    vf = vp.astype(F32)
-                    mean = jnp.mean(vf * vf, axis=-1, keepdims=True)
-                    unit = vf * lax.rsqrt(mean + 1e-6)
-                    if p == 0:
-                        unit = unit * (LOGIT * LOG2E)
-                    vp = unit.astype(BF16)
-                parts.append(vp)
-            whole = jnp.concatenate(parts, axis=1)
-            qkv[h][pl.ds(m * 2, 2)] = whole.reshape(2, TILE, QKV)
-            return carry
-
-        lax.fori_loop(0, TILES // 2, rows, 0)
+            unit = []
+            for p in range(2):
+                vf = (val[:, p * HW:(p + 1) * HW] * rs).astype(BF16).astype(F32)
+                mean = jnp.mean(vf * vf, axis=-1, keepdims=True)
+                unit.append(vf * lax.rsqrt(mean + 1e-6))
+            query = (unit[0] * (LOGIT * LOG2E)).astype(BF16)
+            key = unit[1].astype(BF16)
+            value = (val[:, 2 * HW:] * rs).astype(BF16)
+            row8 = lax.broadcasted_iota(jnp.int32, (8, HW), 0)
+            for i in range(2):
+                t = m * 2 + i
+                part = slice(i * TILE, (i + 1) * TILE)
+                qkv[h][t, :, :HW] = query[part]
+                qkv[h][t, :, HW:2 * HW] = key[part]
+                qkv[h][t, :, 2 * HW:] = value[part]
+                is_late = jnp.broadcast_to(late[h * TILES + t:h * TILES + t + 1, :], (TILE, HW)) > 0
+                msg[h][t, :TILE, :HW] = jnp.where(is_late, query[part], key[part])
+                msg[h][t, :TILE, HW:] = value[part]
+                tot = jnp.sum(unit[1][part], axis=0, keepdims=True)
+                high = tot.astype(BF16).astype(F32)
+                extra = jnp.where(row8 == 0, high, jnp.where(row8 == 1, tot - high, 0.0))
+                msg[h][t, TILE:, :HW] = extra.astype(BF16)
+                msg[h][t, TILE:, HW:] = jnp.zeros((8, HW), BF16)
 
     def a_copy(h, d, recv_side=False):
         dy, dx = d // NX, d % NX
@@ -344,12 +404,18 @@
             device_id=(z, dev), device_id_type=MESH,
         )
 
+    def stage_tiles(h):
+        if h == 0:
+            recv[0][0] = msg[0][t_inv[0, 0]]
+
+        def one(d, carry):
+            stage[h][d] = msg[h][t_inv[h, d]]
+            return carry
+
+        lax.fori_loop(1 - h, NCHIP, one, 0)
+
     def send_tiles(h):
-        if h == 0:
-            recv[0][0] = qkv[0][t_inv[0, 0]]
-
         def one(d, carry):
-            stage[h][d] = qkv[h][t_inv[h, d]]
             a_copy(h, d).start()
             return carry
 
@@ -362,28 +428,47 @@
 
         lax.fori_loop(1 - h, NCHIP, one, 0)
 
+    row = lax.broadcasted_iota(jnp.int32, (TILE, TILE), 0)
+    col = lax.broadcasted_iota(jnp.int32, (TILE, TILE), 1)
+    ones = jnp.ones((TILE, HW), BF16)
+    contract_last = (((1,), (1,)), ((), ()))
+
+    def attend_own(h):
+        def one(t, carry):
+            mine = qkv[h][t]
+            logits = lax.dot_general(
+                mine[:, :HW], mine[:, HW:2 * HW], contract_last, preferred_element_type=F32
+            )
+            probs = jnp.where(col <= row, jnp.exp2(logits), 0.0).astype(BF16)
+            own[h][t] = jnp.dot(
+                probs, jnp.concatenate([mine[:, 2 * HW:], ones], axis=1),
+                preferred_element_type=F32,
+            )
+            return carry
+
+        lax.fori_loop(0, TILES, one, 0)
+
     def attend(h):
-        row = lax.broadcasted_iota(jnp.int32, (TILE, 2 * TILE), 0)
-        col = lax.broadcasted_iota(jnp.int32, (TILE, 2 * TILE), 1)
-        ones = jnp.ones((2 * TILE, HW), BF16)
+        row8 = lax.broadcasted_iota(jnp.int32, (8, TILE), 0)
+        ones8 = jnp.ones((8, TILE), BF16)
 
         def one(d, store):
-            par = t_par[h, d]
-            lim = t_lim[h, d]
-            mine = recv[h][d]
-            other = recv[h][par]
-            keys = jnp.concatenate([mine[:, HW:2 * HW], other[:, HW:2 * HW]], axis=0)
-            vals = jnp.concatenate([mine[:, 2 * HW:], other[:, 2 * HW:]], axis=0)
+            earlier = recv[h][t_par[h, d]]
             logits = lax.dot_general(
-                mine[:, :HW], keys, (((1,), (1,)), ((), ())), preferred_element_type=F32
+                recv[h][d, :TILE, :HW], earlier[:TILE, :HW], contract_last,
+                preferred_element_type=F32,
             )
-            allowed = (col <= row) | ((col >= TILE) & (col < lim))
-            probs = jnp.where(allowed, jnp.exp2(logits), 0.0).astype(BF16)
+            logits = jnp.where(col < t_lim[h, d] - TILE, logits, 0.0)
+            probs = jnp.exp2(logits).astype(BF16)
             both = jnp.dot(
-                probs, jnp.concatenate([vals, ones], axis=1), preferred_element_type=F32
+                probs, jnp.concatenate([earlier[:TILE, HW:], ones], axis=1),
+                preferred_element_type=F32,
             )
-            store[h][d] = (both[:, :HW] / both[:, HW:]).astype(BF16)
-            ksum[h, d] = jnp.sum(mine[:, HW:2 * HW].astype(F32).reshape(16, 8, HW), axis=0)
+            tot = lax.dot_general(ones8, probs, contract_last, preferred_element_type=F32)
+            high = tot.astype(BF16).astype(F32)
+            extra = jnp.where(row8 == 0, high, jnp.where(row8 == 1, tot - high, 0.0))
+            store[h][d, :TILE] = (both[:, :HW] / both[:, HW:]).astype(BF16)
+            store[h][d, TILE:] = extra.astype(BF16)
 
         if h == 0:
             one(0, back)
@@ -402,7 +487,7 @@
             sums, counts = carry
             cl = (t_lab[h, d] + 2) // 2 - 1
             hit = rows8 == cl
-            tot = jnp.sum(ksum[h, d], axis=0, keepdims=True)
+            tot = jnp.sum(recv[h][d, TILE:, :HW].astype(F32), axis=0, keepdims=True)
             sums = sums + jnp.where(hit, jnp.broadcast_to(tot, (8, HW)), 0.0)
             counts = counts + jnp.where(hit, float(TILE), 0.0)
             return sums, counts
@@ -420,7 +505,15 @@
 
         lax.fori_loop(1 - h, NCHIP, one, 0)
         for t in range(TILES):
-            gbuf[h, z, pl.ds(t * TILE, TILE)] = back[h][t_dst[h, t]]
+            far = back[h][t_dst[h, t]]
+            is_late = jnp.broadcast_to(late[h * TILES + t:h * TILES + t + 1, :], (TILE, HW)) > 0
+            weight = lax.dot_general(
+                far[TILE:], jnp.ones((8, HW), BF16), (((0,), (0,)), ((), ())),
+                preferred_element_type=F32,
+            )
+            top = own[h][t, :, :HW] + jnp.where(is_late, weight * far[:TILE].astype(F32), 0.0)
+            low = own[h][t, :, HW:] + jnp.where(is_late, weight, 0.0)
+            gbuf[h, z, pl.ds(t * TILE, TILE)] = (top / low).astype(BF16)
 
     half = TILES * TILE // 2
 
@@ -479,17 +572,30 @@
 
         lax.fori_loop(0, 4, cols, 0)
 
-    project(0)
+    rest = w_steps[1][12 - lag:]
+    for m in range(4):
+        project(0, m)
+        if m < 3 and rest:
+            rest.pop(0)()
+    stage_tiles(0)
     send_tiles(0)
-    project(1)
-    send_tiles(1)
+    for f in rest:
+        f()
+    for m in range(4):
+        project(1, m)
+    stage_tiles(1)
+    attend_own(0)
+    attend_own(1)
     arrivals(0)
     attend(0)
+    send_tiles(1)
     come_home(0)
     z_first(0)
+    z_step(0, 1)
+    z_step(0, 2)
     arrivals(1)
-    z_step(0, 1)
     attend(1)
+    z_step(0, 3)
     centroids(0)
     for j in range(4):
         not_self = (zg != z) | (s % 4 != j)
@@ -499,34 +605,47 @@
             scattered(j).wait_recv()
 
     o_steps[0]()
-    z_step(0, 2)
     o_steps[1]()
     come_home(1)
     z_first(1)
     centroids(1)
-    z_step(0, 3)
-    for f in o_steps[2:]:
-        f()
+    o_steps[2]()
+    o_steps[3]()
+    o_steps[4]()
+    o_steps[5]()
+    z_step(1, 1)
+    o_steps[6]()
+    o_steps[7]()
+    z_step(0, 4)
+    o_steps[8]()
+    o_steps[9]()
+    z_step(1, 2)
+    o_steps[10]()
+    o_steps[11]()
     for g in range(NZ):
         for h in range(2):
             at = (g * 2 + h) * HW
             owt[h, g] = obuf[at:at + HW, :].astype(F32).T.astype(BF16)
-    z_step(1, 1)
-    z_step(0, 4)
     multiply(0, 0, 1, "first")
     multiply(0, 7, 2, "mid")
-    z_step(1, 2)
+    z_step(1, 3)
     multiply(0, 6, 3, "mid")
     multiply(0, 5, 4, "mid")
     multiply(1, 1, 7, "mid")
-    z_step(1, 3)
     multiply(1, 2, 6, "mid")
     multiply(1, 3, 5, "mid")
     z_step(1, 4)
     multiply(1, 0, 4, "last")
 
-    gather_w.drain()
+    gather_w[0].drain()
+    gather_w[1].drain()
     gather_o.drain()
+
+    def codes_sent(i, carry):
+        code_copy(i).wait_send()
+        return carry
+
+    lax.fori_loop(1, NSEQ, codes_sent, 0)
     for i in range(4):
         @pl.when((zg != z) | (s % 4 != i))
         def _(i=i):
@@ -543,7 +662,6 @@
 
 
 def on_device(tokens, qkv_weight, out_weight, centroids, clusters, slots):
-    codes = lax.all_gather(clusters * 2 + slots, "seq", axis=0, tiled=False).reshape(NSEQ, 16)
     vmem = pl.BlockSpec(memory_space=pltpu.VMEM)
     dma = pltpu.SemaphoreType.DMA
     return pl.pallas_call(
@@ -553,7 +671,7 @@
             jax.ShapeDtypeStruct(centroids.shape, F32),
         ),
         in_specs=[
-            pl.BlockSpec(memory_space=pltpu.SMEM),
+            vmem, vmem,
             pl.BlockSpec(memory_space=pl.ANY),
             vmem, vmem, vmem,
         ],
@@ -566,25 +684,28 @@
             pltpu.VMEM((TILES * TILE, 128), F32),
         ]
         + [pltpu.VMEM((TILES, TILE, QKV), BF16)] * 2
-        + [pltpu.VMEM((NCHIP, TILE, QKV), BF16)] * 4
-        + [pltpu.VMEM((NCHIP, TILE, HW), BF16)] * 4
+        + [pltpu.VMEM((NCHIP, MROWS, 2 * HW), BF16)] * 4
+        + [pltpu.VMEM((NCHIP, MROWS, HW), BF16)] * 4
         + [
             pltpu.VMEM((2, NZ, TILES * TILE, HW), BF16),
             pltpu.VMEM((4, OCOLS, 256), F32),
-            pltpu.VMEM((2, NCHIP, 8, HW), F32),
         ]
+        + [pltpu.VMEM((TILES, MROWS, 2 * HW), BF16)] * 2
+        + [pltpu.VMEM((TILES, TILE, 2 * HW), F32)] * 2
+        + [pltpu.VMEM((2 * TILES, 128), jnp.int32)]
+        + [pltpu.SMEM((NSEQ, 2, 128), jnp.int32), pltpu.VMEM((NSEQ, 2, 128), jnp.int32)]
         + [pltpu.SMEM((2, NCHIP), jnp.int32)] * 5
         + [pltpu.SMEM((2, TILES), jnp.int32)]
         + [
-            dma((TILES,)), dma((36,)), dma((36,)), dma((36,)), dma((36,)),
+            dma((TILES,)), dma((2, 36)), dma((2, 36)), dma((36,)), dma((36,)),
             dma((4,)), dma((4,)), dma,
             dma((2, NCHIP)), dma((2, NCHIP)), dma((2, NCHIP)), dma((2, NCHIP)),
-            dma((2, 16)), dma((2, 16)),
+            dma((2, 16)), dma((2, 16)), dma((NSEQ,)), dma((NSEQ,)),
         ],
         compiler_params=pltpu.CompilerParams(
             collective_id=0, has_side_effects=True, vmem_limit_bytes=60 * 1024 * 1024
         ),
-    )(codes, tokens, qkv_weight, out_weight, centroids)
+    )(clusters, slots, tokens, qkv_weight, out_weight, centroids)
 
 
 def solution(mesh):

time: 178 us -> 144 us (0.81)
  blocking collectives: 25.8 us -> 0 us
  Pallas kernels: 146 us -> 140 us
    all_gather x1 -> x0, blocking collectives: 25.8 us -> none  [on_device(): lax.all_gather(clusters * 2 + slots, 'seq', axis=0, tiled=False)]
    pallas_call x1, Pallas kernels: 146 us -> 140 us  [on_device(): pl.pallas_call(kernel, out_shape=(jax.ShapeDtypeStruct((OCOLS, TILES * TI...]
where the time goes in v2:
time: 144 us
  Pallas kernels  140 us (97%)
  local copies, waits for them, and re-layouts  3.56 us (2%)
    pallas_call x1, Pallas kernels, on_device(): pl.pallas_call(kernel, out_shape=(jax.ShapeDtypeStruct((OCOLS, TILES * TI...  140 us
    unnamed x2, local copies, waits for them, and re-layouts  3.56 us

profile of v2, /device:TPU:1, one launch (start us, length us, event | category | flops | bytes accessed | tf_op | source)
XLA Modules:
  0.0 143.8 jit_solution(17381796481647967852)
XLA Ops:
  0.6 139.6 %shard_map.77 = (bf16[512,1024]{1,0:T(8,128)(2,1)}, f32[2,8,128]{2,1,0:T(8,128)}) custom-call(s32[2,8]{1,0:T(2,128)} %clus_ref.1, s32[2,8]{1,0:T(2,128)} %slot_ref.1, bf16[1024,4096]{1,0:T(8,128)(2,1)} %tok_hbm.1, bf16[128,768]{1,0:T(8,128)(2,1)} %w_ref.1, bf16[256,128]{1,0:T(8,128)(2,1)} %wo_ref.1, f32[2,8,128]{2,1,0:T(8,128)} %cent_ref.1), custom_call_target="tpu_custom_call" | custom-call | tf_op jit(solution)/shard_map/pallas_call | solution.py:667
  140.2 2.3 %copy.10 = bf16[512,1024]{1,0:T(8,128)(2,1)} copy(bf16[512,1024]{1,0:T(8,128)(2,1)} %get-tuple-element.4) | data formatting | bytes 2097152
  142.5 1.3 copy.11

commit v3 on v2

--- a/solution.py
+++ b/solution.py
@@ -446,7 +446,7 @@
             )
             return carry
 
-        lax.fori_loop(0, TILES, one, 0)
+        lax.fori_loop(0, TILES, one, 0, unroll=4)
 
     def attend(h):
         row8 = lax.broadcasted_iota(jnp.int32, (8, TILE), 0)
@@ -473,12 +473,16 @@
         if h == 0:
             one(0, back)
 
-        def loop(d, carry):
-            one(d, ret)
-            r_copy(h, d).start()
-            return carry
-
-        lax.fori_loop(1 - h, NCHIP, loop, 0)
+        group = 5 if h == 0 else 4
+
+        def loop(g, carry):
+            for i in range(group):
+                one(1 - h + g * group + i, ret)
+            for i in range(group):
+                r_copy(h, 1 - h + g * group + i).start()
+            return carry
+
+        lax.fori_loop(0, (NCHIP - 1 + h) // group, loop, 0)
 
     def centroids(h):
         rows8 = lax.broadcasted_iota(jnp.int32, (8, HW), 0)
@@ -554,23 +558,17 @@
         ga = (z + ga) % NZ
         gb = (z + gb) % NZ
 
-        def cols(n, carry):
-            at = pl.ds(pl.multiple_of(n * 256, 256), 256)
-            rhs = jnp.concatenate([gbuf[h, ga, at], gbuf[h, gb, at]], axis=1)
-            lhs = jnp.concatenate([owt[h, ga], owt[h, gb]], axis=1)
+        rhs = jnp.concatenate([gbuf[h, ga], gbuf[h, gb]], axis=1)
+        for m in range(2):
+            part = slice(m * 256, (m + 1) * 256)
+            lhs = jnp.concatenate([owt[h, ga, part], owt[h, gb, part]], axis=1)
             val = lax.dot_general(lhs, rhs, (((1,), (1,)), ((), ())), preferred_element_type=F32)
             if mode != "first":
-                val = val + acc[n]
+                val = val + acc[m]
             if mode == "last":
-                for m in range(4):
-                    @pl.when(n == m)
-                    def _(m=m):
-                        out_ref[:, m * 256:(m + 1) * 256] = val.astype(BF16)
+                out_ref[part, :] = val.astype(BF16)
             else:
-                acc[n] = val
-            return carry
-
-        lax.fori_loop(0, 4, cols, 0)
+                acc[m] = val
 
     rest = w_steps[1][12 - lag:]
     for m in range(4):
@@ -586,53 +584,51 @@
     stage_tiles(1)
     attend_own(0)
     attend_own(1)
+    for j in range(4):
+        not_self = (zg != z) | (s % 4 != j)
+
+        @pl.when(not_self)
+        def _(j=j):
+            scattered(j).wait_recv()
+
     arrivals(0)
     attend(0)
     send_tiles(1)
     come_home(0)
     z_first(0)
+    o_steps[0]()
     z_step(0, 1)
+    o_steps[1]()
+    o_steps[2]()
     z_step(0, 2)
+    o_steps[3]()
+    o_steps[4]()
     arrivals(1)
     attend(1)
     z_step(0, 3)
-    centroids(0)
-    for j in range(4):
-        not_self = (zg != z) | (s % 4 != j)
-
-        @pl.when(not_self)
-        def _(j=j):
-            scattered(j).wait_recv()
-
-    o_steps[0]()
-    o_steps[1]()
+    o_steps[5]()
+    o_steps[6]()
+    o_steps[7]()
     come_home(1)
     z_first(1)
+    for f in o_steps[8:]:
+        f()
+    centroids(0)
     centroids(1)
-    o_steps[2]()
-    o_steps[3]()
-    o_steps[4]()
-    o_steps[5]()
-    z_step(1, 1)
-    o_steps[6]()
-    o_steps[7]()
-    z_step(0, 4)
-    o_steps[8]()
-    o_steps[9]()
-    z_step(1, 2)
-    o_steps[10]()
-    o_steps[11]()
     for g in range(NZ):
         for h in range(2):
             at = (g * 2 + h) * HW
             owt[h, g] = obuf[at:at + HW, :].astype(F32).T.astype(BF16)
+    z_step(0, 4)
     multiply(0, 0, 1, "first")
+    z_step(1, 1)
     multiply(0, 7, 2, "mid")
-    z_step(1, 3)
     multiply(0, 6, 3, "mid")
     multiply(0, 5, 4, "mid")
     multiply(1, 1, 7, "mid")
+    z_step(1, 2)
     multiply(1, 2, 6, "mid")
+    z_step(1, 3)
     multiply(1, 3, 5, "mid")
     z_step(1, 4)
     multiply(1, 0, 4, "last")
@@ -688,7 +684,7 @@
         + [pltpu.VMEM((NCHIP, MROWS, HW), BF16)] * 4
         + [
             pltpu.VMEM((2, NZ, TILES * TILE, HW), BF16),
-            pltpu.VMEM((4, OCOLS, 256), F32),
+            pltpu.VMEM((2, 256, TILES * TILE), F32),
         ]
         + [pltpu.VMEM((TILES, MROWS, 2 * HW), BF16)] * 2
         + [pltpu.VMEM((TILES, TILE, 2 * HW), F32)] * 2

time: 144 us -> 134 us (0.931)
  Pallas kernels: 140 us -> 130 us
    pallas_call x1, Pallas kernels: 140 us -> 130 us  [on_device(): pl.pallas_call(kernel, out_shape=(jax.ShapeDtypeStruct((OCOLS, TILES * TI...]
where the time goes in v3:
time: 134 us
  Pallas kernels  130 us (97%)
  local copies, waits for them, and re-layouts  3.56 us (3%)
    pallas_call x1, Pallas kernels, on_device(): pl.pallas_call(kernel, out_shape=(jax.ShapeDtypeStruct((OCOLS, TILES * TI...  130 us
    unnamed x2, local copies, waits for them, and re-layouts  3.56 us

profile of v3, /device:TPU:1, one launch (start us, length us, event | category | flops | bytes accessed | tf_op | source)
XLA Modules:
  0.0 133.8 jit_solution(3764435141061227899)
XLA Ops:
  0.6 129.6 %shard_map.77 = (bf16[512,1024]{1,0:T(8,128)(2,1)}, f32[2,8,128]{2,1,0:T(8,128)}) custom-call(s32[2,8]{1,0:T(2,128)} %clus_ref.1, s32[2,8]{1,0:T(2,128)} %slot_ref.1, bf16[1024,4096]{1,0:T(8,128)(2,1)} %tok_hbm.1, bf16[128,768]{1,0:T(8,128)(2,1)} %w_ref.1, bf16[256,128]{1,0:T(8,128)(2,1)} %wo_ref.1, f32[2,8,128]{2,1,0:T(8,128)} %cent_ref.1), custom_call_target="tpu_custom_call" | custom-call | tf_op jit(solution)/shard_map/pallas_call | solution.py:663
  130.2 2.3 %copy.10 = bf16[512,1024]{1,0:T(8,128)(2,1)} copy(bf16[512,1024]{1,0:T(8,128)(2,1)} %get-tuple-element.4) | data formatting | bytes 2097152
  132.5 1.3 copy.11

commit v4 on v3

--- a/solution.py
+++ b/solution.py
@@ -91,7 +91,7 @@
             rscale[at, :] = jnp.broadcast_to(lax.rsqrt(mean + 1e-5), (16, 128))
             return carry
 
-        lax.fori_loop(0, TILE // 16, rows, 0)
+        lax.fori_loop(0, TILE // 16, rows, 0, unroll=4)
 
     pl.semaphore_wait(barrier, jnp.where(zg != z, NSEQ - 1 + 2 + 4, NSEQ - 1 + 2))
 
@@ -126,11 +126,8 @@
             if k == 1:
                 sl = slot(c, u, v + 1 if recv_side else v)
                 return self.copy(sl, None, slot(c, u, v - 1), 1)
-            if k == 2:
-                sl = slot(c, u, v - 2 if recv_side else v - 1)
-                return self.copy(sl, 0, slot(c, u, v + 1), 2)
-            sl = slot(c, u, v + 2 if recv_side else v + 1)
-            return self.copy(sl, 1, slot(c, u, v - 1), 3)
+            sl = slot(c, u, v + 2 if recv_side else v)
+            return self.copy(sl, None, slot(c, u, v + 2), 2)
 
         def u_copy(self, j, k, recv_side=False):
             vv = v + (0, -1, 1, 2)[j]
@@ -160,15 +157,14 @@
             def first():
                 self.v_copy(0).start()
                 self.v_copy(1).start()
+                self.v_copy(2).start()
                 self.u_copy(0, 0).start()
                 self.u_copy(0, 1).start()
                 self.c_copy(0, 0).start()
 
             def second():
                 self.v_copy(0, True).wait_recv()
-                self.v_copy(2).start()
                 self.v_copy(1, True).wait_recv()
-                self.v_copy(3).start()
                 for j in (1, 2):
                     self.u_copy(j, 0).start()
                     self.u_copy(j, 1).start()
@@ -176,7 +172,6 @@
 
             def third():
                 self.v_copy(2, True).wait_recv()
-                self.v_copy(3, True).wait_recv()
                 self.u_copy(3, 0).start()
                 self.u_copy(3, 1).start()
                 self.c_copy(0, 3).start()
@@ -209,7 +204,7 @@
             ]
 
         def drain(self):
-            for k in range(4):
+            for k in range(3):
                 self.v_copy(k).wait_send()
             for j in range(4):
                 for k in range(4):
@@ -251,10 +246,10 @@
     def codes_read():
         pltpu.make_async_copy(cbuf, codes_ref, loc_sem).wait()
 
-    def lateness():
+    def lateness(h):
         place = lax.broadcasted_iota(jnp.int32, (NSEQ, 128), 0) * TILES
         place = place + lax.broadcasted_iota(jnp.int32, (NSEQ, 128), 1)
-        for h in range(2):
+        if True:
             codes = cbuf[:, h, :]
             for t in range(TILES):
                 mine = own_codes[h:h + 1, t:t + 1]
@@ -300,24 +295,32 @@
             cp.start()
             cp.wait()
 
+    def send_table(h):
+        def per_offset(d, carry):
+            dy, dx = d // NX, d % NX
+            dst = (((y + dy) % NX) * NX + (x + dx) % NX) * 2 + (c + h) % 2
+            inv = jnp.int32(0)
+            for t in range(TILES):
+                mine = codes_ref[s, h, t]
+                inv = jnp.where((mine // 16) == dst, t, inv)
+            t_inv[h, d] = inv
+            return carry
+
+        lax.fori_loop(0, NCHIP, per_offset, 0)
+
     def tables(h):
         def per_offset(d, carry):
             dy, dx = d // NX, d % NX
             src = (((y + NX - dy) % NX) * NX + (x + NX - dx) % NX) * 2 + (c + h) % 2
-            dst = (((y + dy) % NX) * NX + (x + dx) % NX) * 2 + (c + h) % 2
             lab = jnp.int32(-1)
             til = jnp.int32(0)
-            inv = jnp.int32(0)
             for t in range(TILES):
                 code = codes_ref[src, h, t]
                 hit = (code // 16) == s
                 lab = jnp.where(hit, code % 16, lab)
                 til = jnp.where(hit, t, til)
-                mine = codes_ref[s, h, t]
-                inv = jnp.where((mine // 16) == dst, t, inv)
             t_lab[h, d] = lab
             t_tile[h, d] = src * TILES + til
-            t_inv[h, d] = inv
             return carry
 
         lax.fori_loop(0, NCHIP, per_offset, 0)
@@ -351,11 +354,11 @@
             w_steps[1][k - lag]()
         if k == 5:
             codes_here()
-            lateness()
+            lateness(0)
         if k == 8:
             codes_read()
-        if k in (8, 9):
-            tables(k - 8)
+        if k == 8:
+            send_table(0)
 
     def project(h, m):
         if True:
@@ -518,6 +521,9 @@
             top = own[h][t, :, :HW] + jnp.where(is_late, weight * far[:TILE].astype(F32), 0.0)
             low = own[h][t, :, HW:] + jnp.where(is_late, weight, 0.0)
             gbuf[h, z, pl.ds(t * TILE, TILE)] = (top / low).astype(BF16)
+            if t % 4 == 3:
+                for way in range(2):
+                    z_copy(h, way, 1, t // 4).start()
 
     half = TILES * TILE // 2
 
@@ -538,10 +544,6 @@
             return [(way, j) for j in range(2) for way in range(2)]
         return [(0, 0), (1, 1)]
 
-    def z_first(h):
-        for way, j in z_parts(1):
-            z_copy(h, way, 1, j).start()
-
     def z_step(h, k):
         nxt = z_parts(k + 1) if k < 4 else []
         for way, j in z_parts(k):
@@ -577,13 +579,17 @@
             rest.pop(0)()
     stage_tiles(0)
     send_tiles(0)
+    lateness(1)
     for f in rest:
         f()
     for m in range(4):
         project(1, m)
+    send_table(1)
     stage_tiles(1)
     attend_own(0)
+    tables(0)
     attend_own(1)
+    tables(1)
     for j in range(4):
         not_self = (zg != z) | (s % 4 != j)
 
@@ -595,7 +601,6 @@
     attend(0)
     send_tiles(1)
     come_home(0)
-    z_first(0)
     o_steps[0]()
     z_step(0, 1)
     o_steps[1]()
@@ -610,7 +615,6 @@
     o_steps[6]()
     o_steps[7]()
     come_home(1)
-    z_first(1)
     for f in o_steps[8:]:
         f()
     centroids(0)

time: 134 us -> 129 us (0.963)
  Pallas kernels: 130 us -> 124 us
    pallas_call x1, Pallas kernels: 130 us -> 124 us  [on_device(): pl.pallas_call(kernel, out_shape=(jax.ShapeDtypeStruct((OCOLS, TILES * TI...]
where the time goes in v4:
time: 129 us
  Pallas kernels  124 us (96%)
  local copies, waits for them, and re-layouts  3.56 us (3%)
    pallas_call x1, Pallas kernels, on_device(): pl.pallas_call(kernel, out_shape=(jax.ShapeDtypeStruct((OCOLS, TILES * TI...  124 us
    unnamed x2, local copies, waits for them, and re-layouts  3.56 us

profile of v4, /device:TPU:1, one launch (start us, length us, event | category | flops | bytes accessed | tf_op | source)
XLA Modules:
  0.0 128.5 jit_solution(18390429702638248184)
XLA Ops:
  0.6 124.3 %shard_map.77 = (bf16[512,1024]{1,0:T(8,128)(2,1)}, f32[2,8,128]{2,1,0:T(8,128)}) custom-call(s32[2,8]{1,0:T(2,128)} %clus_ref.1, s32[2,8]{1,0:T(2,128)} %slot_ref.1, bf16[1024,4096]{1,0:T(8,128)(2,1)} %tok_hbm.1, bf16[128,768]{1,0:T(8,128)(2,1)} %w_ref.1, bf16[256,128]{1,0:T(8,128)(2,1)} %wo_ref.1, f32[2,8,128]{2,1,0:T(8,128)} %cent_ref.1), custom_call_target="tpu_custom_call" | custom-call | tf_op jit(solution)/shard_map/pallas_call | solution.py:667
  124.9 2.3 %copy.10 = bf16[512,1024]{1,0:T(8,128)(2,1)} copy(bf16[512,1024]{1,0:T(8,128)(2,1)} %get-tuple-element.4) | data formatting | bytes 2097152
  127.2 1.3 %copy.11 = f32[2,8,128]{2,1,0:T(8,128)} copy(f32[2,8,128]{2,1,0:T(8,128)} %get-tuple-element.5) | data formatting | bytes 16384
